TPU v7x, 256 devices: a whole 4x4x8 slice. The times are simulated.
256 devices in a mesh: req: 16 (over y, x_hi, core), blk: 16 (over z, x_lo).
Axes of the slice: x: 4 (x_hi: 2, x_lo: 2; x = x_hi * 2 + x_lo), y: 4, z: 8, core: 2. Of those that a mesh axis runs over, the one named last changes fastest.
Arguments:
- tokens: bfloat16 [32, 256, 1600], P('req'), may hold values from -6 to 6
- cache_kv: bfloat16 [4, 8192, 16, 128], P(None, 'req', 'blk'), may hold values from -500 to 500
- w_qkv: bfloat16 [1600, 16, 192], P(None, 'blk'), may hold values from -0.15625 to 0.15625
- w_out: bfloat16 [16, 64, 1600], P('blk'), may hold values from -0.1875 to 0.1875
- w_fc: bfloat16 [1600, 6400], P(None, 'blk'), may hold values from -0.15625 to 0.15625
- w_proj: bfloat16 [6400, 1600], P('blk'), may hold values from -0.078125 to 0.078125
- embed_table: bfloat16 [50256, 1600], P('req', 'blk'), may hold values from -6 to 6
- group_ids: int32 [32], replicated, may hold values from 0 to 3, never falling along the last dimension, each value on 1 to 16 neighbouring positions
- cache_len: int32 [4], replicated, may hold values from 512 to 8192, as said below
- accept: int32 [2, 32, 256], P(None, 'req'), may hold values 0 or 1
- new_ids: int32 [2, 32, 256], replicated, may hold values from 0 to 50255
Outputs:
- denoised: bfloat16 [32, 256, 1600], P('req')
Inputs may be any that keep to these rules, and one draw needn't show every extreme that they name: `group_ids`: requests of one group stand in consecutive order; each of the 4 groups holds 1 to 16 requests and one holds exactly 16. Cache positions 0 to cache_len[g] - 1 of group g are live; one group's cache is full in every draw.
All inputs are finite; a program needn't handle non-finite values. No bound on the sum of `accept` on one device may be relied on, other than what follows from the above.
Results may differ from a plain program's by a relative error of at most 0.04.
Values may be sent and summed in bfloat16 or wider, within the bound.
A program may use at most 128 MiB of HBM per device.

v0:
```python
import jax
import jax.numpy as jnp
from jax import lax
from jax.sharding import PartitionSpec as P

PASSES = 2


def layer_norm(values):
    centre = values - jnp.mean(values, -1, keepdims=True)
    spread = jnp.mean(centre * centre, -1, keepdims=True)
    return centre * lax.rsqrt(spread + 1e-05)


def attend(projected, own_cache, lengths, head_dim):
    queries = projected[..., :head_dim]
    keys_new = projected[..., head_dim : 2 * head_dim]
    values_new = projected[..., 2 * head_dim :]
    factor = head_dim ** (-0.5)
    scores = (
        jnp.einsum("rqhd,rkhd->rhqk", queries, keys_new, preferred_element_type=jnp.float32)
        * factor
    )
    highest = jnp.max(scores, -1)
    weights_raw = jnp.exp(scores - highest[..., None])
    totals = jnp.sum(weights_raw, -1)
    gathered = jnp.einsum(
        "rhqk,rkhd->rhqd",
        weights_raw.astype(jnp.bfloat16),
        values_new,
        preferred_element_type=jnp.float32,
    )
    cache_size = own_cache.shape[1]
    key_span = min(1024, cache_size)

    def visit_block(block_index, carried):
        highest, totals, gathered = carried
        cache_piece = lax.dynamic_slice_in_dim(own_cache, block_index * key_span, key_span, 1)
        scores = (
            jnp.einsum(
                "rqhd,rkhd->rhqk",
                queries,
                cache_piece[..., :head_dim],
                preferred_element_type=jnp.float32,
            )
            * factor
        )
        position = block_index * key_span + jnp.arange(key_span, dtype=jnp.int32)
        scores = jnp.where(
            position[None, None, None, :] < lengths[:, None, None, None], scores, -1e30
        )
        raised = jnp.maximum(highest, jnp.max(scores, -1))
        shrink = jnp.exp(highest - raised)
        weights_raw = jnp.exp(scores - raised[..., None])
        totals = totals * shrink + jnp.sum(weights_raw, -1)
        gathered = gathered * shrink[..., None] + jnp.einsum(
            "rhqk,rkhd->rhqd",
            weights_raw.astype(jnp.bfloat16),
            cache_piece[..., head_dim:],
            preferred_element_type=jnp.float32,
        )
        return (raised, totals, gathered)

    highest, totals, gathered = lax.fori_loop(
        0, cache_size // key_span, visit_block, (highest, totals, gathered)
    )
    mixed_heads = gathered / totals[..., None]
    return jnp.transpose(mixed_heads, (0, 2, 1, 3)).astype(jnp.bfloat16)


def shards(
    tokens, cache_kv, w_qkv, w_out, w_fc, w_proj, embed_table, group_ids, cache_len, accept, new_ids
):
    req_index = lax.axis_index("req")
    per_device = tokens.shape[0]
    kv_width = cache_kv.shape[3]
    head_dim = kv_width // 2
    my_groups = lax.dynamic_slice_in_dim(group_ids, req_index * per_device, per_device)
    every_cache = lax.all_gather(cache_kv, "req", axis=1, tiled=True)
    own_cache = jnp.take(every_cache, my_groups, axis=0)
    lengths = jnp.take(cache_len, my_groups)
    vocab_dev = embed_table.shape[0]
    relative = new_ids - req_index * vocab_dev
    inside = (relative >= 0) & (relative < vocab_dev)
    looked = jnp.take(embed_table, jnp.clip(relative, 0, vocab_dev - 1), axis=0)
    looked = jnp.where(inside[..., None], looked, jnp.zeros((), jnp.bfloat16))
    picked = (
        lax.psum_scatter(looked, "req", scatter_dimension=1, tiled=True)
        .astype(jnp.float32)
        .astype(jnp.bfloat16)
    )
    fresh_rows = lax.all_gather(picked, "blk", axis=3, tiled=True)
    current = tokens
    for pass_index in range(PASSES):
        state_f32 = current.astype(jnp.float32)
        normed = layer_norm(state_f32).astype(jnp.bfloat16)
        projected = jnp.einsum(
            "rbd,dhc->rbhc", normed, w_qkv, preferred_element_type=jnp.float32
        ).astype(jnp.bfloat16)
        head_rows = attend(projected, own_cache, lengths, head_dim)
        partial_terms = jnp.einsum(
            "rbhc,hcd->rbd", head_rows, w_out, preferred_element_type=jnp.float32
        )
        middle = state_f32 + lax.psum(partial_terms.astype(jnp.bfloat16), "blk").astype(jnp.float32)
        normed_mid = layer_norm(middle).astype(jnp.bfloat16)
        hidden = jax.nn.gelu(
            jnp.einsum("rbd,df->rbf", normed_mid, w_fc, preferred_element_type=jnp.float32),
            approximate=True,
        ).astype(jnp.bfloat16)
        grown_rows = jnp.einsum("rbf,fd->rbd", hidden, w_proj, preferred_element_type=jnp.float32)
        current = (
            middle + lax.psum(grown_rows.astype(jnp.bfloat16), "blk").astype(jnp.float32)
        ).astype(jnp.bfloat16)
        current = jnp.where(accept[pass_index][..., None] == 1, fresh_rows[pass_index], current)
    return current


def solution(mesh):
    return jax.shard_map(
        shards,
        mesh=mesh,
        in_specs=(
            P("req", None, None),
            P(None, "req", "blk", None),
            P(None, "blk", None),
            P("blk", None, None),
            P(None, "blk"),
            P("blk", None),
            P("req", "blk"),
            P(),
            P(),
            P(None, "req", None),
            P(),
        ),
        out_specs=P("req", None, None),
        check_vma=False,
    )
```

profile of v0, /device:TPU:6, one launch (start us, length us, event | category | flops | bytes accessed | tf_op | source)
XLA Modules:
  0.0 969.9 jit_solution(16571325852743032627)
XLA Ops:
  7.3 0.9 compare_and_fusion
  8.2 1.5 copy.29
  9.8 57.4 %gather_fusion = bf16[16384,100]{1,0:T(8,128)(2,1)} fusion(bf16[3141,100]{1,0:T(8,128)(2,1)S(1)} %copy.29, s32[16384]{0:T(1024)S(1)} %broadcast_clamp_fusion), kind=kCustom, calls=%fused_computation | custom fusion | bytes 6619136 | tf_op jit(solution)/shard_map/jit(_take)/gather | solution.py:85
  67.2 7.7 copy.44
  74.9 2.3 select_select_fusion
  77.2 5.1 copy.31
  82.4 1.4 copy-done.2
  86.8 2.7 all-gather.5.cloned.1.call-done
  89.6 5.7 slice_bitcast_fusion.1
  95.3 4.4 gather_fusion.3
  99.6 4.3 gather_fusion.2
  103.9 4.0 maximum_select_fusion
  107.9 6.4 copy.37
  114.4 34.5 %while.34 = (s32[]{:T(128)}, f32[2,1,256]{2,0,1:T(2,128)S(1)}, f32[2,1,256]{2,0,1:T(2,128)S(1)}, f32[2,1,256,64]{2,3,0,1:T(8,128)S(1)}, s32[2]{0:T(128)S(1)}, /*...) while((s32[]{:T(128)}, f32[2,1,256]{2,0,1:T(2,128)S(1)}, ...), condition=%wide.region_8.9_spmd, body=%wide.region_5.8_spmd.sunk | while | flops 140055040 | bytes 7192775 | solution.py:64
  114.4 1.7 bitcast_reduce_fusion.4
  116.8 1.8 fusion.149
  118.8 1.7 bitcast_reduce_fusion.4
  121.1 1.8 fusion.149
  123.1 1.7 bitcast_reduce_fusion.4
  125.4 1.8 fusion.149
  127.4 1.7 bitcast_reduce_fusion.4
  129.7 1.8 fusion.149
  131.7 1.7 bitcast_reduce_fusion.4
  134.1 1.8 fusion.149
  136.0 1.7 bitcast_reduce_fusion.4
  138.4 1.8 fusion.149
  140.3 1.7 bitcast_reduce_fusion.4
  142.7 1.8 fusion.149
  144.7 1.7 bitcast_reduce_fusion.4
  147.0 1.8 fusion.149
  148.9 1.8 convolution_convert_fusion.1
  152.0 92.6 %all-reduce.15.cloned.1.call-done = bf16[2,32,256,100]{2,0,3,1:T(2,128)(2,1)} async-done(((bf16[2,32,256,100]{2,0,3,1:T(2,128)(2,1)}), bf16[2,32,256,100]{2,0,3,1:T(2,128)(2,1)}) %all-reduce.15.cloned.1.call-update) | async-done | bytes 3276816
  244.6 1.1 constant_dynamic-slice_fusion
  245.7 0.9 copy.32
  246.8 147.8 %all-reduce.7.cloned.1.call-done = bf16[2,256,1600]{1,2,0:T(8,128)(2,1)} async-done(((bf16[2,256,1600]{1,2,0:T(8,128)(2,1)}), bf16[2,256,1600]{1,2,0:T(8,128)(2,1)}) %all-reduce.7.cloned.1.call-update) | async-done | bytes 1638416 | tf_op jit(solution)/shard_map/psum | solution.py:104
  394.6 2.0 fusion.38
  397.3 5.1 convolution_convert_fusion.3
  402.5 75.9 %all-gather.3.cloned.1.call-done = bf16[2,2,256,1600]{2,1,0,3:T(2,128)(2,1)} async-done(((bf16[2,2,256,100]{2,1,0,3:T(2,128)(2,1)}), bf16[2,2,256,1600]{2,1,0,3:T(2,128)(2,1)}) %all-gather.3.cloned.1.call-update) | async-done | bytes 3276816 | tf_op jit(solution)/shard_map/all_gather | solution.py:92
  478.4 5.4 fusion.135
  483.8 139.8 %all-reduce.9.cloned.1.call-done = bf16[2,256,1600]{1,2,0:T(8,128)(2,1)} async-done(((bf16[2,256,1600]{1,2,0:T(8,128)(2,1)}), bf16[2,256,1600]{1,2,0:T(8,128)(2,1)}) %all-reduce.9.cloned.1.call-update) | async-done | bytes 1638416 | tf_op jit(solution)/shard_map/psum | solution.py:112
  623.6 3.4 convert_reduce_fusion
  628.8 34.4 %while.35 = (s32[]{:T(128)}, f32[2,1,256]{2,0,1:T(2,128)S(1)}, f32[2,1,256]{2,0,1:T(2,128)S(1)}, f32[2,1,256,64]{2,3,0,1:T(8,128)S(1)}, s32[2]{0:T(128)S(1)}, /*...) while((s32[]{:T(128)}, f32[2,1,256]{2,0,1:T(2,128)S(1)}, ...), condition=%wide.region_20.21_spmd, body=%wide.region_17.20_spmd.sunk | while | flops 140055040 | bytes 7192775 | solution.py:64
  628.9 1.7 bitcast_reduce_fusion.5
  631.3 1.8 fusion.153
  633.2 1.7 bitcast_reduce_fusion.5
  635.6 1.8 fusion.153
  637.5 1.7 bitcast_reduce_fusion.5
  639.9 1.8 fusion.153
  641.8 1.7 bitcast_reduce_fusion.5
  644.2 1.8 fusion.153
  646.1 1.7 bitcast_reduce_fusion.5
  648.5 1.8 fusion.153
  650.4 1.7 bitcast_reduce_fusion.5
  652.8 1.8 fusion.153
  654.7 1.7 bitcast_reduce_fusion.5
  657.1 1.8 fusion.153
  659.0 1.7 bitcast_reduce_fusion.5
  661.4 1.8 fusion.153
  663.3 1.8 convolution_convert_fusion
  665.4 142.6 %all-reduce.11.cloned.1.call-done = bf16[2,256,1600]{1,2,0:T(8,128)(2,1)} async-done(((bf16[2,256,1600]{1,2,0:T(8,128)(2,1)}), bf16[2,256,1600]{1,2,0:T(8,128)(2,1)}) %all-reduce.11.cloned.1.call-update) | async-done | bytes 1638416 | tf_op jit(solution)/shard_map/psum | solution.py:104
  808.0 2.0 fusion.39
  810.6 5.1 convolution_convert_fusion.2
  815.8 142.9 %all-reduce.13.cloned.1.call-done = bf16[2,256,1600]{1,2,0:T(8,128)(2,1)} async-done(((bf16[2,256,1600]{1,2,0:T(8,128)(2,1)}), bf16[2,256,1600]{1,2,0:T(8,128)(2,1)}) %all-reduce.13.cloned.1.call-update) | async-done | bytes 1638416 | tf_op jit(solution)/shard_map/psum | solution.py:112
  958.7 4.4 fusion.43
  (169 shorter events, 20.1 us)
Async XLA Ops:
  6.5 390.8 %copy-start = (bf16[400,1600]{1,0:T(8,128)(2,1)S(1)}, bf16[400,1600]{1,0:T(8,128)(2,1)}, u32[]{:S(2)}) copy-start(bf16[400,1600]{1,0:T(8,128)(2,1)} %param.20) | copy-start | bytes 3840004
  6.5 83.0 %all-gather.5.cloned.1.call-start = ((), (), s32[]{:S(2)}) async-start(), calls=%async_computation.1 | async-start | bytes 8912896 | tf_op jit(solution)/shard_map/all_gather | solution.py:79
  7.3 237.3 %all-reduce.15.cloned.1.call-start = ((), (), s32[]{:S(2)}) async-start(), calls=%async_computation.6 | async-start | bytes 6553600
  82.3 1.4 copy-start.2
  82.3 312.3 %all-reduce.7.cloned.1.call-start = ((), (), s32[]{:S(2)}) async-start(), calls=%async_computation.2 | async-start | bytes 3276800 | tf_op jit(solution)/shard_map/psum | solution.py:104
  83.7 1.1 copy-start.11
  84.8 1.3 copy-start.10
  84.8 1.4 copy-start.1
  85.5 9.8 %copy-start.7 = (bf16[2,256,1,192]{1,3,0,2:T(8,128)(2,1)}, bf16[2,256,1,192]{1,3,0,2:T(8,128)(2,1)S(1)}, u32[]{:S(2)}) copy-start(bf16[2,256,1,192]{1,3,0,2:T(8,128)(2,1)S(1)} %fusion.66) | copy-start | bytes 589828
  107.9 6.4 slice-start
  114.4 34.5 %copy-start.8 = (bf16[1,64,1600]{2,1,0:T(8,128)(2,1)S(1)}, bf16[1,64,1600]{2,1,0:T(8,128)(2,1)}, u32[]{:S(2)}) copy-start(bf16[1,64,1600]{2,1,0:T(8,128)(2,1)} %param.18) | copy-start | bytes 614404
  148.9 1.9 copy-start.13
  150.7 327.7 %all-gather.3.cloned.1.call-start = ((), (), s32[]{:S(2)}) async-start(), calls=%async_computation | async-start | bytes 3481600 | tf_op jit(solution)/shard_map/all_gather | solution.py:92
  246.6 377.0 %all-reduce.9.cloned.1.call-start = ((), (), s32[]{:S(2)}) async-start(), calls=%async_computation.3 | async-start | bytes 3276800 | tf_op jit(solution)/shard_map/psum | solution.py:112
  394.6 2.0 copy-start.5
  397.3 5.2 copy-start.9
  402.5 405.5 %all-reduce.11.cloned.1.call-start = ((), (), s32[]{:S(2)}) async-start(), calls=%async_computation.4 | async-start | bytes 3276800 | tf_op jit(solution)/shard_map/psum | solution.py:104
  623.6 3.9 copy-start.12
  627.0 1.2 copy-start.3
  663.2 144.7 %copy-start.4 = (bf16[2,256,1600]{1,2,0:T(8,128)(2,1)S(1)}, bf16[2,256,1600]{1,2,0:T(8,128)(2,1)}, u32[]{:S(2)}) copy-start(bf16[2,256,1600]{1,2,0:T(8,128)(2,1)} %copy-done.3) | copy-start | bytes 4915204
  665.1 293.6 %all-reduce.13.cloned.1.call-start = ((), (), s32[]{:S(2)}) async-start(), calls=%async_computation.5 | async-start | bytes 3276800 | tf_op jit(solution)/shard_map/psum | solution.py:112
  808.0 2.0 copy-start.6
Sparse Core Ops, SparseCore 0:
  10.1 79.3 all-gather.4
  92.2 152.3 all-reduce.14
  247.3 147.2 all-reduce.6
  396.4 81.9 all-gather.2
  481.1 142.4 all-reduce.8
  665.2 142.7 all-reduce.10
  815.9 142.7 all-reduce.12
where the time goes:
time: 971 us; the launch traced here: 970 us
  waiting for transfers between devices  745 us (77%)
  local copies, waits for them, and re-layouts  103 us (11%)
  matrix products  72.2 us (7%)
  other arithmetic  33.6 us (3%)
  between operations  14.4 us (1%)
    psum x2, waiting for transfers between devices, shards(): lax.psum(partial_terms.astype(jnp.bfloat16), 'blk').astype(jnp.float32)  290 us
    psum x2, waiting for transfers between devices, shards(): lax.psum(grown_rows.astype(jnp.bfloat16), 'blk').astype(jnp.float32)  283 us
    unnamed x8, waiting for transfers between devices  93.4 us
    all_gather x1, waiting for transfers between devices, shards(): fresh_rows = lax.all_gather(picked, 'blk', axis=3, tiled=True)  75.9 us
    gather x2, local copies, waits for them, and re-layouts, shards(): looked = jnp.take(embed_table, jnp.clip(relative, 0, vocab_dev - 1), axis=0)  65.1 us
    dot_general x16, matrix products, visit_block(): jnp.einsum('rhqk,rkhd->rhqd', weights_raw.astype(jnp.bfloat16), cache_pie...  29.2 us
    dot_general x16, matrix products, visit_block(): jnp.einsum('rqhd,rkhd->rhqk', queries, cache_piece[..., :head_dim], prefe...  26.9 us
  transfers between devices with their start and end apart: 7, of which 7 were waited for; matrix products, arithmetic and copies ran while one was open for 16% of the time, Pallas kernels for 0%

commit v1 on v0

--- a/solution.py
+++ b/solution.py
@@ -109,7 +109,10 @@
         ).astype(jnp.bfloat16)
         grown_rows = jnp.einsum("rbf,fd->rbd", hidden, w_proj, preferred_element_type=jnp.float32)
         current = (
-            middle + lax.psum(grown_rows.astype(jnp.bfloat16), "blk").astype(jnp.float32)
+            middle
+            + jnp.sum(lax.all_gather(grown_rows.astype(jnp.bfloat16), "blk"), axis=0).astype(
+                jnp.float32
+            )
         ).astype(jnp.bfloat16)
         current = jnp.where(accept[pass_index][..., None] == 1, fresh_rows[pass_index], current)
     return current

time: 971 us -> 1800 us (1.85)
  waiting for transfers between devices: 745 us -> 1540 us
  other arithmetic: 33.6 us -> 62.8 us
    all_gather x0 -> x2, waiting for transfers between devices: none -> 1080 us  [shards(): lax.all_gather(grown_rows.astype(jnp.bfloat16), 'blk')]
    psum x2 -> x0, waiting for transfers between devices: 283 us -> none  [shards(): lax.psum(grown_rows.astype(jnp.bfloat16), 'blk').astype(jnp.float32)]
    reduce_sum x0 -> x2, other arithmetic: none -> 29.8 us  [shards(): jnp.sum(lax.all_gather(grown_rows.astype(jnp.bfloat16), 'blk'), axis=0)]
  transfers between devices with their start and end apart: 7 -> 7, of which waited for: 7 -> 7; matrix products, arithmetic and copies ran while one was open for 16% -> 9% of each run, Pallas kernels for 0% -> 0%
where the time goes in v1:
time: 1800 us
  waiting for transfers between devices  1540 us (86%)
  local copies, waits for them, and re-layouts  102 us (6%)
  matrix products  83.5 us (5%)
  other arithmetic  62.8 us (3%)
    all_gather x2, waiting for transfers between devices, shards(): lax.all_gather(grown_rows.astype(jnp.bfloat16), 'blk')  1080 us
    psum x2, waiting for transfers between devices, shards(): lax.psum(partial_terms.astype(jnp.bfloat16), 'blk').astype(jnp.float32)  293 us
    unnamed x8, waiting for transfers between devices  90.1 us
    all_gather x1, waiting for transfers between devices, shards(): fresh_rows = lax.all_gather(picked, 'blk', axis=3, tiled=True)  75.9 us
    gather x2, local copies, waits for them, and re-layouts, shards(): looked = jnp.take(embed_table, jnp.clip(relative, 0, vocab_dev - 1), axis=0)  65.1 us
    dot_general x16, matrix products, visit_block(): jnp.einsum('rhqk,rkhd->rhqd', weights_raw.astype(jnp.bfloat16), cache_pie...  36.9 us
  transfers between devices with their start and end apart: 7, of which 7 were waited for; matrix products, arithmetic and copies ran while one was open for 9% of the time, Pallas kernels for 0%

profile of v1, /device:TPU:6, one launch (start us, length us, event | category | flops | bytes accessed | tf_op | source)
XLA Modules:
  0.0 1799.7 jit_solution(6120267539857099011)
XLA Ops:
  8.2 1.5 copy.29
  9.8 57.4 %gather_fusion = bf16[16384,100]{1,0:T(8,128)(2,1)} fusion(bf16[3141,100]{1,0:T(8,128)(2,1)S(1)} %copy.29, s32[16384]{0:T(1024)S(1)} %broadcast_clamp_fusion), kind=kCustom, calls=%fused_computation | custom fusion | bytes 6619136 | tf_op jit(solution)/shard_map/jit(_take)/gather | solution.py:85
  67.2 7.7 copy.44
  74.9 2.3 select_select_fusion
  77.2 5.1 copy.31
  82.4 1.4 copy-done.2
  87.5 2.1 all-gather.9.cloned.1.call-done
  89.6 5.7 slice_bitcast_fusion.1
  95.3 3.1 gather_fusion.2
  98.4 4.3 gather_fusion.3
  102.8 3.7 maximum_select_fusion
  106.4 6.4 copy.37
  112.9 38.1 %while.34 = (s32[]{:T(128)}, f32[2,1,256]{2,0,1:T(2,128)S(1)}, f32[2,1,256]{2,0,1:T(2,128)S(1)}, f32[2,1,256,64]{2,3,0,1:T(8,128)}, s32[2]{0:T(128)S(1)}, /*inde...) while((s32[]{:T(128)}, f32[2,1,256]{2,0,1:T(2,128)S(1)}, ...), condition=%wide.region_8.9_spmd, body=%wide.region_5.8_spmd.sunk | while | flops 140055040 | bytes 7192775 | solution.py:64
  112.9 1.7 bitcast_reduce_fusion.4
  114.6 2.3 fusion.149
  117.7 1.7 bitcast_reduce_fusion.4
  119.4 2.3 fusion.149
  122.5 1.7 bitcast_reduce_fusion.4
  124.2 2.3 fusion.149
  127.2 1.7 bitcast_reduce_fusion.4
  128.9 2.3 fusion.149
  132.0 1.7 bitcast_reduce_fusion.4
  133.7 2.3 fusion.149
  136.8 1.7 bitcast_reduce_fusion.4
  138.5 2.3 fusion.149
  141.5 1.7 bitcast_reduce_fusion.4
  143.2 2.3 fusion.149
  146.3 1.7 bitcast_reduce_fusion.4
  148.0 2.3 fusion.149
  151.0 2.9 convolution_convert_fusion.1
  155.3 89.3 %all-reduce.9.cloned.1.call-done = bf16[2,32,256,100]{2,0,3,1:T(2,128)(2,1)} async-done(((bf16[2,32,256,100]{2,0,3,1:T(2,128)(2,1)}), bf16[2,32,256,100]{2,0,3,1:T(2,128)(2,1)}) %all-reduce.9.cloned.1.call-update) | async-done | bytes 3276816
  244.5 1.1 constant_dynamic-slice_fusion
  246.7 147.8 %all-reduce.5.cloned.1.call-done = bf16[2,256,1600]{1,2,0:T(8,128)(2,1)} async-done(((bf16[2,256,1600]{1,2,0:T(8,128)(2,1)}), bf16[2,256,1600]{1,2,0:T(8,128)(2,1)}) %all-reduce.5.cloned.1.call-update) | async-done | bytes 1638416 | tf_op jit(solution)/shard_map/psum | solution.py:104
  394.5 2.0 fusion.38
  397.3 5.1 convolution_convert_fusion.3
  402.5 75.9 %all-gather.7.cloned.1.call-done = bf16[2,2,256,1600]{2,1,0,3:T(2,128)(2,1)} async-done(((bf16[2,2,256,100]{2,1,0,3:T(2,128)(2,1)}), bf16[2,2,256,1600]{2,1,0,3:T(2,128)(2,1)}) %all-gather.7.cloned.1.call-update) | async-done | bytes 3276816 | tf_op jit(solution)/shard_map/all_gather | solution.py:92
  478.4 5.3 fusion.135
  483.7 535.7 %all-gather.11.cloned.1.call-done = bf16[32,256,1600]{1,2,0:T(8,128)(2,1)} async-done(((bf16[2,256,1600]{1,2,0:T(8,128)(2,1)}), bf16[32,256,1600]{1,2,0:T(8,128)(2,1)}) %all-gather.11.cloned.1.call-update) | async-done | bytes 26214416 | tf_op jit(solution)/shard_map/all_gather | solution.py:113
  1019.4 14.9 reduce_sum.150
  1034.4 3.4 convert_reduce_fusion
  1040.2 38.1 %while.35 = (s32[]{:T(128)}, f32[2,1,256]{2,0,1:T(2,128)S(1)}, f32[2,1,256]{2,0,1:T(2,128)S(1)}, f32[2,1,256,64]{2,3,0,1:T(8,128)}, s32[2]{0:T(128)S(1)}, /*inde...) while((s32[]{:T(128)}, f32[2,1,256]{2,0,1:T(2,128)S(1)}, ...), condition=%wide.region_20.21_spmd, body=%wide.region_17.20_spmd.sunk | while | flops 140055040 | bytes 7192775 | solution.py:64
  1040.3 1.7 bitcast_reduce_fusion.5
  1042.0 2.3 fusion.153
  1045.1 1.7 bitcast_reduce_fusion.5
  1046.8 2.3 fusion.153
  1049.8 1.7 bitcast_reduce_fusion.5
  1051.5 2.3 fusion.153
  1054.6 1.7 bitcast_reduce_fusion.5
  1056.3 2.3 fusion.153
  1059.4 1.7 bitcast_reduce_fusion.5
  1061.1 2.3 fusion.153
  1064.1 1.7 bitcast_reduce_fusion.5
  1065.8 2.3 fusion.153
  1068.9 1.7 bitcast_reduce_fusion.5
  1070.6 2.3 fusion.153
  1073.7 1.7 bitcast_reduce_fusion.5
  1075.4 2.3 fusion.153
  1078.3 2.9 convolution_convert_fusion
  1081.6 144.8 %all-reduce.7.cloned.1.call-done = bf16[2,256,1600]{1,2,0:T(8,128)(2,1)} async-done(((bf16[2,256,1600]{1,2,0:T(8,128)(2,1)}), bf16[2,256,1600]{1,2,0:T(8,128)(2,1)}) %all-reduce.7.cloned.1.call-update) | async-done | bytes 1638416 | tf_op jit(solution)/shard_map/psum | solution.py:104
  1226.3 2.0 fusion.39
  1229.0 5.1 convolution_convert_fusion.2
  1234.1 539.4 %all-gather.13.cloned.1.call-done = bf16[32,256,1600]{1,2,0:T(8,128)(2,1)} async-done(((bf16[2,256,1600]{1,2,0:T(8,128)(2,1)}), bf16[32,256,1600]{1,2,0:T(8,128)(2,1)}) %all-gather.13.cloned.1.call-update) | async-done | bytes 26214416 | tf_op jit(solution)/shard_map/all_gather | solution.py:113
  1773.5 14.9 reduce_sum.157
  1788.5 4.4 fusion.43
  (171 shorter events, 22.9 us)
Async XLA Ops:
  6.5 390.7 %copy-start = (bf16[400,1600]{1,0:T(8,128)(2,1)S(1)}, bf16[400,1600]{1,0:T(8,128)(2,1)}, u32[]{:S(2)}) copy-start(bf16[400,1600]{1,0:T(8,128)(2,1)} %param.20) | copy-start | bytes 3840004
  6.5 83.0 %all-gather.9.cloned.1.call-start = ((), (), s32[]{:S(2)}) async-start(), calls=%async_computation.1 | async-start | bytes 8912896 | tf_op jit(solution)/shard_map/all_gather | solution.py:79
  7.3 237.3 %all-reduce.9.cloned.1.call-start = ((), (), s32[]{:S(2)}) async-start(), calls=%async_computation.6 | async-start | bytes 6553600
  82.3 1.4 copy-start.2
  82.3 312.2 %all-reduce.5.cloned.1.call-start = ((), (), s32[]{:S(2)}) async-start(), calls=%async_computation.2 | async-start | bytes 3276800 | tf_op jit(solution)/shard_map/psum | solution.py:104
  83.7 1.1 copy-start.11
  84.8 1.9 copy-start.10
  84.8 2.0 copy-start.1
  85.4 1.3 copy-start.8
  106.4 6.4 slice-start
  151.0 3.0 copy-start.13
  151.0 243.6 %copy-start.3 = (bf16[2,256,1600]{1,2,0:T(8,128)(2,1)S(1)}, bf16[2,256,1600]{1,2,0:T(8,128)(2,1)}, u32[]{:S(2)}) copy-start(bf16[2,256,1600]{1,2,0:T(8,128)(2,1)} %param.15) | copy-start | bytes 4915204
  153.9 324.4 %all-gather.7.cloned.1.call-start = ((), (), s32[]{:S(2)}) async-start(), calls=%async_computation | async-start | bytes 3481600 | tf_op jit(solution)/shard_map/all_gather | solution.py:92
  246.5 773.0 %all-gather.11.cloned.1.call-start = ((), (), s32[]{:S(2)}) async-start(), calls=%async_computation.4 | async-start | bytes 27852800 | tf_op jit(solution)/shard_map/all_gather | solution.py:113
  394.5 2.0 copy-start.6
  397.2 5.2 copy-start.9
  402.4 823.9 %all-reduce.7.cloned.1.call-start = ((), (), s32[]{:S(2)}) async-start(), calls=%async_computation.3 | async-start | bytes 3276800 | tf_op jit(solution)/shard_map/psum | solution.py:104
  1034.4 3.9 copy-start.12
  1037.8 1.2 copy-start.4
  1078.3 148.0 %copy-start.5 = (bf16[2,256,1600]{1,2,0:T(8,128)(2,1)S(1)}, bf16[2,256,1600]{1,2,0:T(8,128)(2,1)}, u32[]{:S(2)}) copy-start(bf16[2,256,1600]{1,2,0:T(8,128)(2,1)} %copy-done.4) | copy-start | bytes 4915204
  1081.3 692.3 %all-gather.13.cloned.1.call-start = ((), (), s32[]{:S(2)}) async-start(), calls=%async_computation.5 | async-start | bytes 27852800 | tf_op jit(solution)/shard_map/all_gather | solution.py:113
  1226.3 2.0 copy-start.7
Sparse Core Ops, SparseCore 0:
  10.1 79.3 all-gather.8
  92.2 152.2 all-reduce.8
  247.2 147.2 all-reduce.4
  396.3 81.9 all-gather.6
  480.1 539.2 all-gather.10
  1081.4 144.8 all-reduce.6
  1234.3 539.2 all-gather.12
